TPU v7x, 32 devices: a whole 2x2x4 slice. The times are simulated.
32 devices in a mesh: pipe: 4 (over x, core), seq: 8 (over z, y).
Axes of the slice: x: 2, y: 2, z: 4, core: 2. Of those that a mesh axis runs over, the one named last changes fastest.
Arguments:
- value_in: bfloat16 [4, 1024, 4096], P('pipe', 'seq'), may hold values from -6 to 6
- gate_one: bfloat16 [4, 1024, 4096], P('pipe', 'seq'), may hold values from -6 to 6
- gate_two: bfloat16 [4, 1024, 4096], P('pipe', 'seq'), may hold values from -6 to 6
- out_grad: bfloat16 [4, 1024, 4096], P('pipe', 'seq'), may hold values from -6 to 6
- w_embed: float32 [4, 33, 64], P('pipe'), may hold values from -1 to 1
- b_embed: float32 [4, 64], P('pipe'), may hold values from -4 to 4
- w_filter: float32 [4, 64, 4096], P('pipe', None, 'seq'), may hold values from -0.75 to 0.75
- decay: float32 [4, 4096], P('pipe', 'seq'), may hold values from 0.3 to 128
- skip: float32 [4, 4096], P('pipe', 'seq'), may hold values from -4 to 4
Outputs:
- next_input: bfloat16 [4, 1024, 4096], P('pipe', 'seq')
- grad_value: bfloat16 [4, 1024, 4096], P('pipe', 'seq')
- grad_gate_one: bfloat16 [4, 1024, 4096], P('pipe', 'seq')
- grad_gate_two: bfloat16 [4, 1024, 4096], P('pipe', 'seq')
- grad_w_embed: float32 [4, 33, 64], P('pipe')
- grad_b_embed: float32 [4, 64], P('pipe')
- grad_w_filter: float32 [4, 64, 4096], P('pipe', None, 'seq')
- grad_decay: float32 [4, 4096], P('pipe', 'seq')
- grad_skip: float32 [4, 4096], P('pipe', 'seq')
All inputs are finite; a program needn't handle non-finite values.
Results may differ from a plain program's by a relative error of at most 0.0058.
Values may be sent and summed in bfloat16 or wider, within the bound.
A program may use at most 128 MiB of HBM per device.

v0:
```python
import math
import jax
import jax.numpy as jnp
from jax import lax
from jax.sharding import PartitionSpec as P

E = 33


def from_behind(value, axis, steps):
    count = lax.axis_size(axis)
    pairs = [(source, (source + steps) % count) for source in range(count)]
    return lax.ppermute(value, axis, pairs)


def contract(form, left, right):
    return jnp.einsum(form, left, right, precision=lax.Precision.HIGHEST)


def position_features(length):
    position_ids = jnp.arange(length, dtype=jnp.int32)
    band_count = (E - 1) // 2
    band_index = jnp.arange(1, band_count + 1, dtype=jnp.int32)
    turn_ids = band_index[:, None] * band_index[:, None] * position_ids[None, :] % length
    angles = 2.0 * math.pi / length * turn_ids.astype(jnp.float32)
    position_ramp = position_ids.astype(jnp.float32)[None, :] / length
    return jnp.concatenate([position_ramp, jnp.cos(angles), jnp.sin(angles)], axis=0)


def build_tables(length):
    fft_total = 2 * length
    outer_len = 128
    half_len = outer_len // 2
    kept_len = half_len + 1
    inner_len = fft_total // outer_len
    index_kept = jnp.arange(kept_len, dtype=jnp.int32)
    index_half = jnp.arange(half_len, dtype=jnp.int32)
    index_inner = jnp.arange(inner_len, dtype=jnp.int32)
    angle_outer = (
        2.0
        * math.pi
        / outer_len
        * (index_kept[:, None] * index_half[None, :] % outer_len).astype(jnp.float32)
    )
    cos_outer = jnp.cos(angle_outer)
    sin_outer = jnp.sin(angle_outer)
    table_first = jnp.concatenate([cos_outer, -sin_outer], axis=0)
    angle_twist = (
        2.0
        * math.pi
        / fft_total
        * (index_kept[:, None] * index_inner[None, :] % fft_total).astype(jnp.float32)
    )
    cos_twist = jnp.cos(angle_twist)[:, :, None]
    sin_twist = jnp.sin(angle_twist)[:, :, None]
    angle_inner = (
        2.0
        * math.pi
        / inner_len
        * (index_inner[:, None] * index_inner[None, :] % inner_len).astype(jnp.float32)
    )
    cos_inner = jnp.cos(angle_inner)
    sin_inner = jnp.sin(angle_inner)
    table_second = jnp.stack(
        [jnp.stack([cos_inner, sin_inner], axis=1), jnp.stack([-sin_inner, cos_inner], axis=1)],
        axis=0,
    )
    table_back = jnp.stack(
        [jnp.stack([cos_inner, -sin_inner], axis=1), jnp.stack([sin_inner, cos_inner], axis=1)],
        axis=0,
    )
    weight_kept = (
        jnp.where((index_kept == 0) | (index_kept == half_len), 1.0, 2.0).astype(jnp.float32)
        / fft_total
    )
    table_last = jnp.stack(
        [
            jnp.transpose(cos_outer) * weight_kept[None, :],
            -jnp.transpose(sin_outer) * weight_kept[None, :],
        ],
        axis=1,
    )
    return (
        table_first,
        cos_twist,
        sin_twist,
        table_second,
        table_back,
        table_last,
        half_len,
        kept_len,
        inner_len,
    )


def staged_forward(field, tables_all):
    (
        table_first,
        cos_twist,
        sin_twist,
        table_second,
        table_back,
        table_last,
        half_len,
        kept_len,
        inner_len,
    ) = tables_all
    columns = field.shape[1]
    shaped = field.reshape(half_len, inner_len, columns)
    stacked = contract("kn,npc->kpc", table_first, shaped)
    part_re = stacked[:kept_len]
    part_im = stacked[kept_len:]
    twisted = jnp.stack(
        [part_re * cos_twist + part_im * sin_twist, part_im * cos_twist - part_re * sin_twist],
        axis=0,
    )
    return contract("sqrp,rkpc->skqc", table_second, twisted)


def staged_inverse(spec, tables_all):
    (
        table_first,
        cos_twist,
        sin_twist,
        table_second,
        table_back,
        table_last,
        half_len,
        kept_len,
        inner_len,
    ) = tables_all
    columns = spec.shape[3]
    sectioned = contract("sprq,rkqc->skpc", table_back, spec)
    section_re = sectioned[0]
    section_im = sectioned[1]
    twisted = jnp.stack(
        [
            section_re * cos_twist - section_im * sin_twist,
            section_im * cos_twist + section_re * sin_twist,
        ],
        axis=0,
    )
    result = contract("nrk,rkpc->npc", table_last, twisted)
    return result.reshape(half_len * inner_len, columns)


def dense_tables(length):
    block = 128
    fine = jnp.arange(block, dtype=jnp.int32)
    coarse = jnp.arange(length // block, dtype=jnp.int32) * block
    point = jnp.arange(length, dtype=jnp.int32)
    unit = math.pi / (2 * length)

    def pair(count):
        angle = unit * (count % (4 * length)).astype(jnp.float32)
        return (jnp.cos(angle), jnp.sin(angle))

    def joined(first, second):
        (cos_f, sin_f), (cos_s, sin_s) = (first, second)
        cos_j = cos_s[:, None, :] * cos_f[None] - sin_s[:, None, :] * sin_f[None]
        sin_j = sin_s[:, None, :] * cos_f[None] + cos_s[:, None, :] * sin_f[None]
        return (cos_j.reshape(length, length), sin_j.reshape(length, length))

    odd = 2 * point + 1
    cos_k, sin_k = joined(
        pair((2 * fine + 1)[:, None] * point[None, :]), pair((2 * coarse)[:, None] * point[None, :])
    )
    ahead = jnp.concatenate([cos_k, -sin_k], axis=0).astype(jnp.bfloat16)
    cos_n, sin_n = joined(pair(fine[:, None] * odd[None, :]), pair(coarse[:, None] * odd[None, :]))
    back = (jnp.concatenate([cos_n, -sin_n], axis=1) * (1.0 / length)).astype(jnp.bfloat16)
    return (ahead, back)


def dense_forward(field, tables_all):
    spec = jnp.dot(tables_all[0], field.astype(jnp.bfloat16), preferred_element_type=jnp.float32)
    return spec.reshape(2, field.shape[0], field.shape[1])


def dense_inverse(spec, tables_all):
    flat = spec.reshape(2 * spec.shape[1], spec.shape[2])
    return jnp.dot(tables_all[1], flat.astype(jnp.bfloat16), preferred_element_type=jnp.float32)


def spectral_product(left, right, conjugate_left):
    left_re = left[0]
    left_im = left[1]
    right_re = right[0]
    right_im = right[1]
    if conjugate_left:
        left_im = -left_im
    return jnp.stack(
        [left_re * right_re - left_im * right_im, left_re * right_im + left_im * right_re], axis=0
    )


def per_device(value_in, gate_one, gate_two, out_grad, w_embed, b_embed, w_filter, decay, skip):
    values = value_in[0]
    gate_first = gate_one[0]
    gate_second = gate_two[0]
    cotangent = out_grad[0]
    filter_w = w_filter[0]
    shards = lax.axis_size("seq")
    length = values.shape[0] * shards
    weighted = (values.astype(jnp.float32) * gate_first.astype(jnp.float32)).astype(jnp.bfloat16)
    upstream = (cotangent.astype(jnp.float32) * gate_second.astype(jnp.float32)).astype(
        jnp.bfloat16
    )
    features = position_features(length)
    preact = contract("ef,et->ft", w_embed[0], features) + b_embed[0][:, None]
    activation = jnp.sin(preact)
    positions = jnp.arange(length, dtype=jnp.int32).astype(jnp.float32)[:, None]
    envelope = jnp.exp(-decay[0][None, :] * positions / length) * (1.0 / math.sqrt(length))
    kernel = contract("ft,fc->tc", activation, filter_w) * envelope
    if length <= 1024 and length % 128 == 0:
        tables_all = dense_tables(length)
        forward_transform, inverse_transform = (dense_forward, dense_inverse)
    else:
        tables_all = build_tables(length)
        forward_transform, inverse_transform = (staged_forward, staged_inverse)
    kernel_spec = forward_transform(kernel, tables_all)
    skip_row = skip[0][None, :]
    weighted_chan, upstream_chan = (
        lax.all_to_all(weighted, "seq", split_axis=1, concat_axis=0, tiled=True),
        lax.all_to_all(upstream, "seq", split_axis=1, concat_axis=0, tiled=True),
    )
    weighted_f = weighted_chan.astype(jnp.float32)
    weighted_spec = forward_transform(weighted_f, tables_all)
    conv = inverse_transform(spectral_product(kernel_spec, weighted_spec, False), tables_all)
    mixed_chan, weighted_f, weighted_spec = (
        (conv + skip_row * weighted_f).astype(jnp.bfloat16),
        weighted_f,
        weighted_spec,
    )
    upstream_f = upstream_chan.astype(jnp.float32)
    upstream_spec = forward_transform(upstream_f, tables_all)
    backward_conv = inverse_transform(
        spectral_product(kernel_spec, upstream_spec, True), tables_all
    )
    grad_chan = (backward_conv + skip_row * upstream_f).astype(jnp.bfloat16)
    grad_skip = jnp.sum(upstream_f * weighted_f, axis=0)
    grad_kernel = inverse_transform(
        spectral_product(weighted_spec, upstream_spec, True), tables_all
    )
    grad_chan, grad_skip, grad_kernel = (grad_chan, grad_skip, grad_kernel)
    mixed_seq, grad_weighted = (
        lax.all_to_all(mixed_chan, "seq", split_axis=0, concat_axis=1, tiled=True),
        lax.all_to_all(grad_chan, "seq", split_axis=0, concat_axis=1, tiled=True),
    )
    output = (gate_second.astype(jnp.float32) * mixed_seq.astype(jnp.float32)).astype(jnp.bfloat16)
    next_input = from_behind(output, "pipe", 1)
    grad_decay = jnp.sum(grad_kernel * kernel * (-positions / length), axis=0)
    grad_raw = grad_kernel * envelope
    grad_filter_w = contract("ft,tc->fc", activation, grad_raw)
    grad_preact = contract("fc,tc->ft", filter_w, grad_raw) * jnp.cos(preact)
    part_weight = contract("et,ft->ef", features, grad_preact)
    part_bias = jnp.sum(grad_preact, axis=1)
    grad_embed_w, grad_embed_b = lax.psum((part_weight, part_bias), "seq")
    grad_values = (grad_weighted.astype(jnp.float32) * gate_first.astype(jnp.float32)).astype(
        jnp.bfloat16
    )
    grad_first = (grad_weighted.astype(jnp.float32) * values.astype(jnp.float32)).astype(
        jnp.bfloat16
    )
    grad_second = (cotangent.astype(jnp.float32) * mixed_seq.astype(jnp.float32)).astype(
        jnp.bfloat16
    )
    moved_values, moved_first, moved_second = from_behind(
        (grad_values, grad_first, grad_second), "pipe", -1
    )
    return (
        next_input[None],
        moved_values[None],
        moved_first[None],
        moved_second[None],
        grad_embed_w[None],
        grad_embed_b[None],
        grad_filter_w[None],
        grad_decay[None],
        grad_skip[None],
    )


def solution(mesh):
    return jax.shard_map(
        per_device,
        mesh=mesh,
        in_specs=(
            P("pipe", "seq", None),
            P("pipe", "seq", None),
            P("pipe", "seq", None),
            P("pipe", "seq", None),
            P("pipe", None, None),
            P("pipe", None),
            P("pipe", None, "seq"),
            P("pipe", "seq"),
            P("pipe", "seq"),
        ),
        out_specs=(
            P("pipe", "seq", None),
            P("pipe", "seq", None),
            P("pipe", "seq", None),
            P("pipe", "seq", None),
            P("pipe", None, None),
            P("pipe", None),
            P("pipe", None, "seq"),
            P("pipe", "seq"),
            P("pipe", "seq"),
        ),
        check_vma=False,
    )
```

profile of v0, /device:TPU:0, one launch (start us, length us, event | category | flops | bytes accessed | tf_op | source)
XLA Modules:
  0.0 202.9 jit_solution(786132404300499328)
XLA Ops:
  0.6 0.0 copy-start
  0.7 1.8 fusion.10
  2.5 0.4 copy.27
  2.9 1.3 copy.20
  4.2 7.3 %all-to-all-start.2 = ((bf16[128,8,512]{2,0,1:T(8,128)(2,1)}), bf16[128,8,512]{2,0,1:T(8,128)(2,1)S(1)}, u32[]{:S(2)}, u32[]{:S(2)}) async-start(bf16[128,8,512]{2,0,1:T(8,128)(2,1)} %copy.20), calls=%async_computation.2 | async-start | bytes 2097152 | tf_op jit(solution)/shard_map/all_to_all | solution.py:224
  11.6 0.2 fusion.3
  11.8 0.3 copy-done.23
  12.2 0.4 copy.26
  12.6 1.3 copy.18
  13.9 0.2 fusion.79
  14.1 0.2 fusion.81
  14.3 0.3 fusion.72
  14.7 1.9 fusion.95
  16.6 3.2 %fusion.54 = (f32[128,1024]{1,0:T(8,128)}, f32[128,1024]{1,0:T(8,128)}) fusion(s32[128]{0:T(128)S(1)} %multiply_add_fusion.1), kind=kLoop, calls=%fused_computation.84 | loop fusion | flops 1835008 | bytes 1049088 | tf_op jit(solution)/shard_map/cos | solution.py:156
  19.8 2.0 %fusion.56 = (f32[128,1024]{1,0:T(8,128)S(1)}, f32[128,1024]{1,0:T(8,128)S(1)}) fusion(s32[1024]{0:T(1024)S(1)} %multiply_add_fusion), kind=kLoop, calls=%fused_computation.86 | loop fusion | flops 1835008 | bytes 1052672 | tf_op jit(solution)/shard_map/cos | solution.py:156
  21.8 3.5 %fusion.12 = f32[1024,512]{1,0:T(8,128)} fusion(f32[1024,64]{0,1:T(8,128)S(1)} %get-tuple-element.46, f32[1024]{0:T(1024)S(1)} %iota_convert_fusion, f32[512]{0:T(512)S(1)} %bitcast.129, f32[1,64,512]{2,1,0:T(8,128)S(1)} %copy-done), kind=kOutput, calls=%fused_computation.40 | convolution fusion | flops 404750336 | bytes 2496512 | tf_op jit(solution)/shard_map/ft,fc->tc/dot_general | solution.py:17
  25.3 11.9 %all-to-all-done.2 = bf16[128,8,512]{2,0,1:T(8,128)(2,1)S(1)} async-done(((bf16[128,8,512]{2,0,1:T(8,128)(2,1)}), bf16[128,8,512]{2,0,1:T(8,128)(2,1)S(1)}, u32[]{:S(2)}, u32[]{:S(2)}) %all-to-all-start.2) | async-done | bytes 1048608 | tf_op jit(solution)/shard_map/all_to_all | solution.py:224
  37.2 3.7 %all-to-all-start = ((bf16[128,8,512]{2,0,1:T(8,128)(2,1)}), bf16[128,8,512]{2,0,1:T(8,128)(2,1)S(1)}, u32[]{:S(2)}, u32[]{:S(2)}) async-start(bf16[128,8,512]{2,0,1:T(8,128)(2,1)} %copy.18), calls=%async_computation | async-start | bytes 2097152 | tf_op jit(solution)/shard_map/all_to_all | solution.py:223
  41.0 2.4 %subtract_convert_fusion = (bf16[8,128,1024]{2,1,0:T(8,128)(2,1)S(1)}, bf16[8,128,1024]{2,1,0:T(8,128)(2,1)S(1)}) fusion(f32[128,1024]{1,0:T(8,128)} %get-tuple-element.45, f32[8,1024]{1,0:T(8,128)S(1)} %get-tuple-element.43, f32[128,1024]{1,0:T(8,128)} %get-tuple-element.44, f32[8,1024]{1,0:T(8,128)S(1)} %get-tuple-element.42), kind=kLoop, calls=%fused_computation.4 | loop fusion | flops 9437184 | bytes 5308416 | tf_op jit(solution)/shard_map/convert.23
  43.5 4.5 %multiply_subtract_fusion = (f32[8,128,1024]{2,1,0:T(8,128)}, f32[8,128,1024]{2,1,0:T(8,128)}) fusion(f32[128,1024]{1,0:T(8,128)S(1)} %get-tuple-element.39, f32[8,1024]{1,0:T(8,128)S(1)} %get-tuple-element.37, f32[128,1024]{1,0:T(8,128)S(1)} %get-tuple-element.38, f32[8,1024]{1,0:T(8,128)S(1)} %get-tuple-element.36), kind=kLoop, calls=%fused_computation.6 | loop fusion | flops 7340032 | bytes 9502720 | tf_op jit(solution)/shard_map/sub | solution.py:160
  47.9 4.4 %fusion.19 = f32[2048,512]{1,0:T(8,128)} fusion(bf16[1024,1024]{1,0:T(8,128)(2,1)S(1)} %bitcast.122, bf16[1024,1024]{1,0:T(8,128)(2,1)S(1)} %bitcast.119, f32[1024,512]{1,0:T(8,128)S(1)} %copy-done.28), kind=kOutput, calls=%fused_computation.45 | convolution fusion | flops 2156396544 | bytes 10485760 | tf_op jit(solution)/shard_map/dot_general | solution.py:175
  52.3 4.5 %fusion.17 = f32[2048,512]{1,0:T(8,128)} fusion(bf16[1024,512]{1,0:T(8,128)(2,1)S(1)} %bitcast.111, bf16[1024,1024]{1,0:T(8,128)(2,1)S(1)} %bitcast.123, bf16[1024,1024]{1,0:T(8,128)(2,1)S(1)} %bitcast.120), kind=kOutput, calls=%fused_computation.43 | convolution fusion | flops 2155872256 | bytes 9437184 | tf_op jit(solution)/shard_map/dot_general | solution.py:175
  56.8 10.1 %all-to-all-done = bf16[128,8,512]{2,0,1:T(8,128)(2,1)S(1)} async-done(((bf16[128,8,512]{2,0,1:T(8,128)(2,1)}), bf16[128,8,512]{2,0,1:T(8,128)(2,1)S(1)}, u32[]{:S(2)}, u32[]{:S(2)}) %all-to-all-start) | async-done | bytes 1048608 | tf_op jit(solution)/shard_map/all_to_all | solution.py:223
  66.8 5.0 %fusion.18 = f32[2048,512]{1,0:T(8,128)S(1)} fusion(bf16[1024,512]{1,0:T(8,128)(2,1)S(1)} %bitcast.113, bf16[1024,1024]{1,0:T(8,128)(2,1)} %bitcast.124, bf16[1024,1024]{1,0:T(8,128)(2,1)} %bitcast.121), kind=kOutput, calls=%fused_computation.44 | convolution fusion | flops 2155872256 | bytes 9437184 | tf_op jit(solution)/shard_map/dot_general | solution.py:175
  71.8 0.1 copy-done.2
  71.9 1.9 fusion.30
  73.9 1.7 pad_maximum_fusion.1
  75.6 1.2 copy-done.3
  76.8 1.3 copy-done.6
  78.1 3.3 %add_convert_fusion.3 = bf16[1024,512]{1,0:T(8,128)(2,1)} fusion(bf16[1024,512]{1,0:T(8,128)(2,1)S(1)} %bitcast.114, bf16[2048,512]{1,0:T(8,128)(2,1)S(1)} %bitcast.125, f32[512]{0:T(512)S(1)} %bitcast.134, f32[1024,1024]{1,0:T(8,128)S(1)} %bitcast.106, f32[1024,1024]{1,0:T(8,128)S(1)} %bitcast.103), kind=kOutput, calls=%fused_computation.35 | convolution fusion | flops 2155872256 | bytes 12584960 | tf_op jit(solution)/shard_map/dot_general | solution.py:181
  81.4 3.8 %all-to-all-start.1 = ((bf16[8,128,512]{2,1,0:T(8,128)(2,1)}), bf16[8,128,512]{2,1,0:T(8,128)(2,1)S(1)}, u32[]{:S(2)}, u32[]{:S(2)}) async-start(bf16[8,128,512]{2,1,0:T(8,128)(2,1)} %bitcast.15), calls=%async_computation.1 | async-start | bytes 2097152 | tf_op jit(solution)/shard_map/all_to_all | solution.py:246
  85.2 4.8 %fusion.28 = (bf16[1,1024,512]{2,1,0:T(8,128)(2,1)S(1)}, bf16[1,1024,512]{2,1,0:T(8,128)(2,1)S(1)}) fusion(f32[2048,512]{1,0:T(8,128)} %fusion.17, f32[2048,512]{1,0:T(8,128)} %fusion.19), kind=kLoop, calls=%fused_computation.52 | loop fusion | flops 4718592 | bytes 10485760 | tf_op jit(solution)/shard_map/stack | solution.py:191
  90.0 0.2 pad_maximum_fusion.2
  90.2 2.0 copy-done.4
  92.2 3.3 %add_convert_fusion.1 = bf16[1024,512]{1,0:T(8,128)(2,1)} fusion(bf16[1024,512]{1,0:T(8,128)(2,1)S(1)} %bitcast.112, bf16[2048,512]{1,0:T(8,128)(2,1)S(1)} %bitcast.117, f32[512]{0:T(512)S(1)} %bitcast.135, f32[1024,1024]{1,0:T(8,128)S(1)} %bitcast.107, f32[1024,1024]{1,0:T(8,128)S(1)} %bitcast.104), kind=kOutput, calls=%fused_computation.32 | convolution fusion | flops 2155872256 | bytes 12584960 | tf_op jit(solution)/shard_map/dot_general | solution.py:181
  95.5 15.5 %all-to-all-done.1 = bf16[8,128,512]{2,1,0:T(8,128)(2,1)S(1)} async-done(((bf16[8,128,512]{2,1,0:T(8,128)(2,1)}), bf16[8,128,512]{2,1,0:T(8,128)(2,1)S(1)}, u32[]{:S(2)}, u32[]{:S(2)}) %all-to-all-start.1) | async-done | bytes 1048608 | tf_op jit(solution)/shard_map/all_to_all | solution.py:246
  111.0 3.6 %all-to-all-start.3 = ((bf16[8,128,512]{2,1,0:T(8,128)(2,1)}), bf16[8,128,512]{2,1,0:T(8,128)(2,1)S(1)}, u32[]{:S(2)}, u32[]{:S(2)}) async-start(bf16[8,128,512]{2,1,0:T(8,128)(2,1)} %bitcast.127), calls=%async_computation.3 | async-start | bytes 2097152 | tf_op jit(solution)/shard_map/all_to_all | solution.py:247
  114.6 0.3 convert_bitcast_fusion.5
  114.9 0.2 copy.24
  115.1 1.0 copy-done.11
  116.1 0.3 copy-done.12
  116.4 1.9 fusion.7
  118.3 22.3 %all-to-all-done.3 = bf16[8,128,512]{2,1,0:T(8,128)(2,1)S(1)} async-done(((bf16[8,128,512]{2,1,0:T(8,128)(2,1)}), bf16[8,128,512]{2,1,0:T(8,128)(2,1)S(1)}, u32[]{:S(2)}, u32[]{:S(2)}) %all-to-all-start.3) | async-done | bytes 1048608 | tf_op jit(solution)/shard_map/all_to_all | solution.py:247
  140.5 0.3 convert_bitcast_fusion.4
  140.8 0.2 copy.25
  141.1 0.7 copy-done.14
  141.8 0.3 copy-done.16
  142.1 1.9 fusion.2
  143.9 1.6 collective-permute-start.1
  145.5 0.0 collective-permute-start.3
  145.6 0.5 collective-permute-start
  146.1 0.1 copy-done.17
  146.1 4.4 %multiply_reduce_fusion.1 = (f32[512]{0:T(512)}, f32[1024,512]{1,0:T(8,128)S(1)}) fusion(f32[1024,512]{1,0:T(8,128)} %fusion.12, f32[1024]{0:T(1024)S(1)} %negate_multiply_fusion, bf16[2048,512]{1,0:T(8,128)(2,1)S(1)} %bitcast.118, f32[1024,1024]{1,0:T(8,128)S(1)} %bitcast.108, f32[1024,1024]{1,0:T(8,128)S(1)} %bitcast.105), kind=kOutput, calls=%fused_computation.29 | convolution fusion | flops 2155347456 | bytes 14686208 | tf_op jit(solution)/shard_map/dot_general | solution.py:181
  150.5 3.3 %fusion.96 = (f32[64]{0:T(128)S(1)}, f32[1024,64]{0,1:T(8,128)S(1)}) fusion(f32[1024,64]{0,1:T(8,128)S(1)} %copy-done.21, f32[1,64,512]{2,1,0:T(8,128)S(1)} %copy-done, f32[1024,512]{1,0:T(8,128)S(1)} %get-tuple-element.51, f32[1024]{0:T(1024)S(1)} %iota_convert_fusion, f32[512]{0:T(512)S(1)} %bitcast.130), kind=kOutput, calls=%fused_computation.143 | convolution fusion | flops 404881344 | bytes 2758912 | tf_op jit(solution)/shard_map/fc,tc->ft/dot_general | solution.py:17
  153.9 0.4 convolution_bitcast_fusion
  154.2 35.7 %all-reduce = (f32[1,33,64]{2,1,0:T(8,128)S(1)}, f32[1,64]{1,0:T(1,128)}) all-reduce(f32[1,33,64]{2,1,0:T(8,128)S(1)} %convolution_bitcast_fusion, f32[1,64]{1,0:T(1,128)S(1)} %bitcast.133), channel_id=1, replica_groups=mesh['pipe'=4,'seq'=8] {'seq'}, use_global_device_ids=true, to_apply=%region_0.1 | all-reduce | flops 2176 | bytes 17408 | tf_op jit(solution)/shard_map/psum | solution.py:257
  190.0 0.6 copy.22
  190.6 1.0 multiply_reduce_fusion
  191.5 0.0 copy-done.27
  191.5 3.4 %fusion.23 = f32[1,64,512]{2,1,0:T(8,128)} fusion(f32[1024,64]{0,1:T(8,128)} %copy-done.20, f32[1024,512]{1,0:T(8,128)S(1)} %copy-done.27, f32[1024]{0:T(1024)S(1)} %iota_convert_fusion, f32[512]{0:T(512)S(1)} %bitcast.131), kind=kOutput, calls=%fused_computation.48 | convolution fusion | flops 404750336 | bytes 2496512 | tf_op jit(solution)/shard_map/ft,tc->fc/dot_general | solution.py:17
  195.0 2.3 %copy.38 = bf16[1,128,4096]{2,1,0:T(8,128)(2,1)} copy(bf16[1,128,4096]{2,1,0:T(8,128)(2,1)} %bitcast.17) | data formatting | bytes 2097152
  197.3 2.3 %copy.39 = bf16[1,128,4096]{2,1,0:T(8,128)(2,1)} copy(bf16[1,128,4096]{2,1,0:T(8,128)(2,1)} %bitcast.27) | data formatting | bytes 2097152
  199.6 1.0 copy.40
  200.6 2.3 %copy.41 = bf16[1,128,4096]{2,1,0:T(8,128)(2,1)} copy(bf16[1,128,4096]{2,1,0:T(8,128)(2,1)} %bitcast.31) | data formatting | bytes 2097152
  (60 shorter events, 0.2 us)
Async XLA Ops:
  0.6 21.2 %copy-start = (f32[1,64,512]{2,1,0:T(8,128)S(1)}, f32[1,64,512]{2,1,0:T(8,128)}, u32[]{:S(2)}) copy-start(f32[1,64,512]{2,1,0:T(8,128)} %param.15) | copy-start | bytes 393220
  2.9 8.6 %copy-start.13 = (bf16[1,128,4096]{2,1,0:T(8,128)(2,1)S(1)}, bf16[1,128,4096]{2,1,0:T(8,128)(2,1)}, u32[]{:S(2)}) copy-start(bf16[1,128,4096]{2,1,0:T(8,128)(2,1)} %param.10) | copy-start | bytes 3145732
  2.9 8.6 %copy-start.15 = (bf16[1,128,4096]{2,1,0:T(8,128)(2,1)S(1)}, bf16[1,128,4096]{2,1,0:T(8,128)(2,1)}, u32[]{:S(2)}) copy-start(bf16[1,128,4096]{2,1,0:T(8,128)(2,1)} %param.9) | copy-start | bytes 3145732
  4.2 33.0 %all-to-all-start.2 = ((bf16[128,8,512]{2,0,1:T(8,128)(2,1)}), bf16[128,8,512]{2,0,1:T(8,128)(2,1)S(1)}, u32[]{:S(2)}, u32[]{:S(2)}) async-start(bf16[128,8,512]{2,0,1:T(8,128)(2,1)} %copy.20), calls=%async_computation.2 | async-start | bytes 2097152 | tf_op jit(solution)/shard_map/all_to_all | solution.py:224
  11.5 0.7 copy-start.23
  12.2 2.5 %copy-start.22 = (f32[1,33,64]{2,0,1:T(1,128)S(1)}, f32[1,33,64]{2,0,1:T(1,128)}, u32[]{:S(2)}) copy-start(f32[1,33,64]{2,0,1:T(1,128)} %param.13) | copy-start | bytes 25348
  12.2 2.5 %copy-start.24 = (f32[1,64]{1,0:T(1,128)S(1)}, f32[1,64]{1,0:T(1,128)}, u32[]{:S(2)}) copy-start(f32[1,64]{1,0:T(1,128)} %param.14) | copy-start | bytes 772
  16.6 5.3 %copy-start.20 = (f32[1024,64]{0,1:T(8,128)}, f32[1024,64]{0,1:T(8,128)S(1)}, u32[]{:S(2)}) copy-start(f32[1024,64]{0,1:T(8,128)S(1)} %get-tuple-element.46) | copy-start | bytes 786436
  37.2 29.6 %all-to-all-start = ((bf16[128,8,512]{2,0,1:T(8,128)(2,1)}), bf16[128,8,512]{2,0,1:T(8,128)(2,1)S(1)}, u32[]{:S(2)}, u32[]{:S(2)}) async-start(bf16[128,8,512]{2,0,1:T(8,128)(2,1)} %copy.18), calls=%async_computation | async-start | bytes 2097152 | tf_op jit(solution)/shard_map/all_to_all | solution.py:223
  43.4 8.9 %copy-start.18 = (bf16[8,128,1024]{2,1,0:T(8,128)(2,1)}, bf16[8,128,1024]{2,1,0:T(8,128)(2,1)S(1)}, u32[]{:S(2)}) copy-start(bf16[8,128,1024]{2,1,0:T(8,128)(2,1)S(1)} %get-tuple-element.34) | copy-start | bytes 6291460
  43.4 8.9 %copy-start.19 = (bf16[8,128,1024]{2,1,0:T(8,128)(2,1)}, bf16[8,128,1024]{2,1,0:T(8,128)(2,1)S(1)}, u32[]{:S(2)}) copy-start(bf16[8,128,1024]{2,1,0:T(8,128)(2,1)S(1)} %get-tuple-element.35) | copy-start | bytes 6291460
  43.4 4.5 %copy-start.28 = (f32[1024,512]{1,0:T(8,128)S(1)}, f32[1024,512]{1,0:T(8,128)}, u32[]{:S(2)}) copy-start(f32[1024,512]{1,0:T(8,128)} %fusion.12) | copy-start | bytes 6291460
  66.8 8.8 %copy-start.9 = (bf16[128,8,512]{2,0,1:T(8,128)(2,1)}, bf16[128,8,512]{2,0,1:T(8,128)(2,1)S(1)}, u32[]{:S(2)}) copy-start(bf16[128,8,512]{2,0,1:T(8,128)(2,1)S(1)} %all-to-all-done) | copy-start | bytes 3145732
  66.8 5.0 %copy-start.1 = (f32[2048,512]{1,0:T(8,128)S(1)}, f32[2048,512]{1,0:T(8,128)}, u32[]{:S(2)}) copy-start(f32[2048,512]{1,0:T(8,128)} %fusion.19) | copy-start | bytes 12582916
  66.8 5.1 %copy-start.2 = (f32[2048,512]{1,0:T(8,128)S(1)}, f32[2048,512]{1,0:T(8,128)}, u32[]{:S(2)}) copy-start(f32[2048,512]{1,0:T(8,128)} %fusion.17) | copy-start | bytes 12582916
  73.9 2.9 %copy-start.3 = (f32[8,128,1024]{2,1,0:T(8,128)S(1)}, f32[8,128,1024]{2,1,0:T(8,128)}, u32[]{:S(2)}) copy-start(f32[8,128,1024]{2,1,0:T(8,128)} %get-tuple-element.32) | copy-start | bytes 12582916
  73.9 4.2 %copy-start.6 = (f32[8,128,1024]{2,1,0:T(8,128)S(1)}, f32[8,128,1024]{2,1,0:T(8,128)}, u32[]{:S(2)}) copy-start(f32[8,128,1024]{2,1,0:T(8,128)} %get-tuple-element.33) | copy-start | bytes 12582916
  73.9 4.2 %copy-start.25 = (f32[1,512]{1,0:T(1,128)S(1)}, f32[1,512]{1,0:T(1,128)}, u32[]{:S(2)}) copy-start(f32[1,512]{1,0:T(1,128)} %param.17) | copy-start | bytes 6148
  81.4 29.6 %all-to-all-start.1 = ((bf16[8,128,512]{2,1,0:T(8,128)(2,1)}), bf16[8,128,512]{2,1,0:T(8,128)(2,1)S(1)}, u32[]{:S(2)}, u32[]{:S(2)}) async-start(bf16[8,128,512]{2,1,0:T(8,128)(2,1)} %bitcast.15), calls=%async_computation.1 | async-start | bytes 2097152 | tf_op jit(solution)/shard_map/all_to_all | solution.py:246
  85.2 5.0 %copy-start.7 = (f32[8,128,1024]{2,1,0:T(8,128)S(1)}, f32[8,128,1024]{2,1,0:T(8,128)}, u32[]{:S(2)}) copy-start(f32[8,128,1024]{2,1,0:T(8,128)} %get-tuple-element.33) | copy-start | bytes 12582916
  90.0 2.2 %copy-start.4 = (f32[8,128,1024]{2,1,0:T(8,128)S(1)}, f32[8,128,1024]{2,1,0:T(8,128)}, u32[]{:S(2)}) copy-start(f32[8,128,1024]{2,1,0:T(8,128)} %get-tuple-element.32) | copy-start | bytes 12582916
  111.0 29.5 %all-to-all-start.3 = ((bf16[8,128,512]{2,1,0:T(8,128)(2,1)}), bf16[8,128,512]{2,1,0:T(8,128)(2,1)S(1)}, u32[]{:S(2)}, u32[]{:S(2)}) async-start(bf16[8,128,512]{2,1,0:T(8,128)(2,1)} %bitcast.127), calls=%async_computation.3 | async-start | bytes 2097152 | tf_op jit(solution)/shard_map/all_to_all | solution.py:247
  114.9 1.2 copy-start.11
  114.9 1.5 copy-start.12
  140.5 1.2 copy-start.14
  140.5 1.5 copy-start.16
  140.8 5.2 %copy-start.8 = (f32[8,128,1024]{2,1,0:T(8,128)S(1)}, f32[8,128,1024]{2,1,0:T(8,128)}, u32[]{:S(2)}) copy-start(f32[8,128,1024]{2,1,0:T(8,128)} %get-tuple-element.33) | copy-start | bytes 12582916
  142.1 4.0 %copy-start.5 = (f32[8,128,1024]{2,1,0:T(8,128)S(1)}, f32[8,128,1024]{2,1,0:T(8,128)}, u32[]{:S(2)}) copy-start(f32[8,128,1024]{2,1,0:T(8,128)} %get-tuple-element.32) | copy-start | bytes 12582916
  142.1 4.0 %copy-start.17 = (bf16[2,1024,512]{2,1,0:T(8,128)(2,1)S(1)}, bf16[2,1024,512]{2,1,0:T(8,128)(2,1)}, u32[]{:S(2)}) copy-start(bf16[2,1024,512]{2,1,0:T(8,128)(2,1)} %get-tuple-element.53) | copy-start | bytes 6291460
  143.9 51.1 %collective-permute-start.2 = (bf16[128,4096]{1,0:T(8,128)(2,1)}, bf16[128,4096]{1,0:T(8,128)(2,1)S(1)}, u32[]{:S(2)}, u32[]{:S(2)}) collective-permute-start(bf16[128,4096]{1,0:T(8,128)(2,1)} %get-tuple-element.30), channel_id=1, source_target_pairs={{0,24},{8,0},{16,8},{24,16},{1,25},{9,1},{17,9},{25,17},{2,26},{10... | collective-permute-start | bytes 3145736 | tf_op jit(solution)/shard_map/ppermute | solution.py:13
  143.9 51.1 %collective-permute-start.1 = (bf16[128,4096]{1,0:T(8,128)(2,1)}, bf16[128,4096]{1,0:T(8,128)(2,1)}, u32[]{:S(2)}, u32[]{:S(2)}) collective-permute-start(bf16[128,4096]{1,0:T(8,128)(2,1)} %get-tuple-element.31), channel_id=1, source_target_pairs={{0,24},{8,0},{16,8},{24,16},{1,25},{9,1},{17,9},{25,17},{2,26},{10... | collective-permute-start | bytes 3145736 | tf_op jit(solution)/shard_map/ppermute | solution.py:13
  145.5 49.5 %collective-permute-start.3 = (bf16[128,4096]{1,0:T(8,128)(2,1)}, bf16[128,4096]{1,0:T(8,128)(2,1)}, u32[]{:S(2)}, u32[]{:S(2)}) collective-permute-start(bf16[128,4096]{1,0:T(8,128)(2,1)} %get-tuple-element.28), channel_id=1, source_target_pairs={{0,24},{8,0},{16,8},{24,16},{1,25},{9,1},{17,9},{25,17},{2,26},{10... | collective-permute-start | bytes 3145736 | tf_op jit(solution)/shard_map/ppermute | solution.py:13
  145.6 49.4 %collective-permute-start = (bf16[128,4096]{1,0:T(8,128)(2,1)}, bf16[128,4096]{1,0:T(8,128)(2,1)}, u32[]{:S(2)}, u32[]{:S(2)}) collective-permute-start(bf16[128,4096]{1,0:T(8,128)(2,1)} %get-tuple-element.29), channel_id=1, source_target_pairs={{0,8},{8,16},{16,24},{24,0},{1,9},{9,17},{17,25},{25,1},{2,10},{10... | collective-permute-start | bytes 3145736 | tf_op jit(solution)/shard_map/ppermute | solution.py:13
  146.1 4.4 %copy-start.21 = (f32[1024,64]{0,1:T(8,128)S(1)}, f32[1024,64]{0,1:T(8,128)}, u32[]{:S(2)}) copy-start(f32[1024,64]{0,1:T(8,128)} %get-tuple-element.47) | copy-start | bytes 786436
  150.5 3.7 %copy-start.26 = (f32[1024,512]{1,0:T(8,128)}, f32[1024,512]{1,0:T(8,128)S(1)}, u32[]{:S(2)}) copy-start(f32[1024,512]{1,0:T(8,128)S(1)} %get-tuple-element.51) | copy-start | bytes 6291460
  150.5 40.1 %copy-start.10 = (bf16[128,8,512]{2,0,1:T(8,128)(2,1)S(1)}, bf16[128,8,512]{2,0,1:T(8,128)(2,1)}, u32[]{:S(2)}) copy-start(bf16[128,8,512]{2,0,1:T(8,128)(2,1)} %copy-done.9) | copy-start | bytes 3145732
  189.9 1.6 copy-start.27
where the time goes:
time: 204 us; the launch traced here: 203 us
  waiting for transfers between devices  59.8 us (29%)
  matrix products  37.4 us (18%)
  blocking collectives  35.7 us (18%)
  other arithmetic  28.9 us (14%)
  starting transfers between devices  20.5 us (10%)
  local copies, waits for them, and re-layouts  19.6 us (10%)
    psum x1, blocking collectives, per_device(): grad_embed_w, grad_embed_b = lax.psum((part_weight, part_bias), 'seq')  35.7 us
    all_to_all x1, waiting for transfers between devices, per_device(): lax.all_to_all(grad_chan, 'seq', split_axis=0, concat_axis=1, tiled=True)  22.3 us
    unnamed x65, local copies, waits for them, and re-layouts  16.6 us
    all_to_all x1, waiting for transfers between devices, per_device(): lax.all_to_all(mixed_chan, 'seq', split_axis=0, concat_axis=1, tiled=True)  15.5 us
    dot_general x3, matrix products, dense_forward(): jnp.dot(tables_all[0], field.astype(jnp.bfloat16), preferred_element_type...  13.8 us
    dot_general x5, matrix products, contract(): return jnp.einsum(form, left, right, precision=lax.Precision.HIGHEST)  12.5 us
    all_to_all x1, waiting for transfers between devices, per_device(): lax.all_to_all(upstream, 'seq', split_axis=1, concat_axis=0, tiled=True)  11.9 us
    dot_general x3, matrix products, dense_inverse(): jnp.dot(tables_all[1], flat.astype(jnp.bfloat16), preferred_element_type=...  11 us
  transfers between devices with their start and end apart: 8, of which 4 were waited for; matrix products, arithmetic and copies ran while one was open for 26% of the time, Pallas kernels for 0%

commit v1 on v0

--- a/solution.py
+++ b/solution.py
@@ -5,6 +5,12 @@
 from jax.sharding import PartitionSpec as P
 
 E = 33
+
+
+def swap_blocks(x, mesh_axis, split, join):
+    pieces = jnp.split(x, lax.axis_size(mesh_axis), axis=split)
+    received = lax.all_to_all(jnp.stack(pieces), mesh_axis, 0, 0)
+    return jnp.concatenate(received, axis=join)
 
 
 def from_behind(value, axis, steps):
@@ -243,7 +249,7 @@
     )
     grad_chan, grad_skip, grad_kernel = (grad_chan, grad_skip, grad_kernel)
     mixed_seq, grad_weighted = (
-        lax.all_to_all(mixed_chan, "seq", split_axis=0, concat_axis=1, tiled=True),
+        swap_blocks(mixed_chan, "seq", 0, 1),
         lax.all_to_all(grad_chan, "seq", split_axis=0, concat_axis=1, tiled=True),
     )
     output = (gate_second.astype(jnp.float32) * mixed_seq.astype(jnp.float32)).astype(jnp.bfloat16)

time: 204 us -> 218 us (1.069)
  local copies, waits for them, and re-layouts: 19.6 us -> 32 us
  waiting for transfers between devices: 59.8 us -> 54.6 us
  other arithmetic: 28.9 us -> 31.9 us
  matrix products: 37.4 us -> 40 us
    all_to_all x1, waiting for transfers between devices: 22.3 us -> 13.2 us  [per_device(): lax.all_to_all(grad_chan, 'seq', split_axis=0, concat_axis=1, tiled=True)]
    unnamed x65, local copies, waits for them, and re-layouts: 16.6 us -> 24.7 us
    all_to_all x1, waiting for transfers between devices: 15.5 us -> 21.9 us  [swap_blocks(): received = lax.all_to_all(jnp.stack(pieces), mesh_axis, 0, 0)]
    another operation x4, other arithmetic: 8.64 us -> 5.35 us  [spectral_product(): jnp.stack([left_re * right_re - left_im * right_im, left_re * right_im +...]
    convert_element_type x0 -> x1, other arithmetic: none -> 2.88 us  [per_device(): mixed_seq.astype(jnp.float32)]
    convert_element_type x1, local copies, waits for them, and re-layouts: 0.17 us -> 2.9 us  [per_device(): mixed_seq.astype(jnp.float32)]
    dot_general x3, matrix products: 11 us -> 13.7 us  [dense_inverse(): jnp.dot(tables_all[1], flat.astype(jnp.bfloat16), preferred_element_type=...]
  transfers between devices with their start and end apart: 8 -> 8, of which waited for: 4 -> 4; matrix products, arithmetic and copies ran while one was open for 26% -> 31% of each run, Pallas kernels for 0% -> 0%
where the time goes in v1:
time: 218 us; the launch traced here: 217 us
  waiting for transfers between devices  54.6 us (25%)
  matrix products  40 us (18%)
  blocking collectives  36.3 us (17%)
  local copies, waits for them, and re-layouts  32 us (15%)
  other arithmetic  31.9 us (15%)
  starting transfers between devices  21.6 us (10%)
    psum x1, blocking collectives, per_device(): grad_embed_w, grad_embed_b = lax.psum((part_weight, part_bias), 'seq')  36.3 us
    unnamed x65, local copies, waits for them, and re-layouts  24.7 us
    all_to_all x1, waiting for transfers between devices, swap_blocks(): received = lax.all_to_all(jnp.stack(pieces), mesh_axis, 0, 0)  21.9 us
    dot_general x3, matrix products, dense_forward(): jnp.dot(tables_all[0], field.astype(jnp.bfloat16), preferred_element_type...  13.8 us
    dot_general x3, matrix products, dense_inverse(): jnp.dot(tables_all[1], flat.astype(jnp.bfloat16), preferred_element_type=...  13.7 us
    all_to_all x1, waiting for transfers between devices, per_device(): lax.all_to_all(grad_chan, 'seq', split_axis=0, concat_axis=1, tiled=True)  13.2 us
    dot_general x5, matrix products, contract(): return jnp.einsum(form, left, right, precision=lax.Precision.HIGHEST)  12.6 us
    all_to_all x1, waiting for transfers between devices, per_device(): lax.all_to_all(upstream, 'seq', split_axis=1, concat_axis=0, tiled=True)  9.81 us
  transfers between devices with their start and end apart: 8, of which 4 were waited for; matrix products, arithmetic and copies ran while one was open for 31% of the time, Pallas kernels for 0%

profile of v1, /device:TPU:0, one launch (start us, length us, event | category | flops | bytes accessed | tf_op | source)
XLA Modules:
  0.0 217.4 jit_solution(6561853705585109339)
XLA Ops:
  0.7 1.7 copy.22
  2.4 0.7 copy.25
  3.1 0.3 fusion.10
  3.3 1.3 copy.26
  4.7 7.3 %all-to-all-start.2 = ((bf16[128,8,512]{2,0,1:T(8,128)(2,1)}), bf16[128,8,512]{2,0,1:T(8,128)(2,1)S(1)}, u32[]{:S(2)}, u32[]{:S(2)}) async-start(bf16[128,8,512]{2,0,1:T(8,128)(2,1)} %copy.26), calls=%async_computation.2 | async-start | bytes 2097152 | tf_op jit(solution)/shard_map/all_to_all | solution.py:230
  12.0 1.8 fusion.3
  13.9 0.4 copy.33
  14.3 1.3 copy.23
  15.5 0.2 fusion.87
  15.8 0.2 fusion.89
  16.0 0.3 fusion.80
  16.4 1.9 fusion.103
  18.3 3.2 %fusion.54 = (f32[128,1024]{1,0:T(8,128)}, f32[128,1024]{1,0:T(8,128)}) fusion(s32[128]{0:T(128)S(1)} %multiply_add_fusion.1), kind=kLoop, calls=%fused_computation.84 | loop fusion | flops 1835008 | bytes 1049088 | tf_op jit(solution)/shard_map/cos | solution.py:162
  21.5 2.9 %fusion.56 = (f32[128,1024]{1,0:T(8,128)}, f32[128,1024]{1,0:T(8,128)}) fusion(s32[1024]{0:T(1024)S(1)} %multiply_add_fusion), kind=kLoop, calls=%fused_computation.86 | loop fusion | flops 1835008 | bytes 1052672 | tf_op jit(solution)/shard_map/cos | solution.py:162
  24.4 3.5 %fusion.12 = f32[1024,512]{1,0:T(8,128)} fusion(f32[1024,64]{0,1:T(8,128)S(1)} %get-tuple-element.55, f32[1024]{0:T(1024)S(1)} %iota_convert_fusion, f32[512]{0:T(512)S(1)} %bitcast.156, f32[1,64,512]{2,1,0:T(8,128)S(1)} %copy-done), kind=kOutput, calls=%fused_computation.40 | convolution fusion | flops 404750336 | bytes 2496512 | tf_op jit(solution)/shard_map/ft,fc->tc/dot_general | solution.py:23
  27.9 9.8 %all-to-all-done.2 = bf16[128,8,512]{2,0,1:T(8,128)(2,1)S(1)} async-done(((bf16[128,8,512]{2,0,1:T(8,128)(2,1)}), bf16[128,8,512]{2,0,1:T(8,128)(2,1)S(1)}, u32[]{:S(2)}, u32[]{:S(2)}) %all-to-all-start.2) | async-done | bytes 1048608 | tf_op jit(solution)/shard_map/all_to_all | solution.py:230
  37.7 4.4 %all-to-all-start = ((bf16[128,8,512]{2,0,1:T(8,128)(2,1)}), bf16[128,8,512]{2,0,1:T(8,128)(2,1)}, u32[]{:S(2)}, u32[]{:S(2)}) async-start(bf16[128,8,512]{2,0,1:T(8,128)(2,1)} %copy.23), calls=%async_computation | async-start | bytes 2097152 | tf_op jit(solution)/shard_map/all_to_all | solution.py:229
  42.2 2.5 %subtract_convert_fusion = (bf16[8,128,1024]{2,1,0:T(8,128)(2,1)S(1)}, bf16[8,128,1024]{2,1,0:T(8,128)(2,1)S(1)}) fusion(f32[128,1024]{1,0:T(8,128)} %get-tuple-element.54, f32[8,1024]{1,0:T(8,128)S(1)} %get-tuple-element.52, f32[128,1024]{1,0:T(8,128)} %get-tuple-element.53, f32[8,1024]{1,0:T(8,128)S(1)} %get-tuple-element.51), kind=kLoop, calls=%fused_computation.4 | loop fusion | flops 9437184 | bytes 5308416 | tf_op jit(solution)/shard_map/convert.23
  44.7 4.4 %multiply_subtract_fusion = (f32[8,128,1024]{2,1,0:T(8,128)}, f32[8,128,1024]{2,1,0:T(8,128)}) fusion(f32[128,1024]{1,0:T(8,128)S(1)} %copy-done.11, f32[8,1024]{1,0:T(8,128)S(1)} %get-tuple-element.46, f32[128,1024]{1,0:T(8,128)S(1)} %copy-done.10, f32[8,1024]{1,0:T(8,128)S(1)} %get-tuple-element.45), kind=kLoop, calls=%fused_computation.6 | loop fusion | flops 7340032 | bytes 9502720 | tf_op jit(solution)/shard_map/sub | solution.py:166
  49.1 4.4 %fusion.19 = f32[2048,512]{1,0:T(8,128)} fusion(bf16[1024,1024]{1,0:T(8,128)(2,1)S(1)} %bitcast.148, bf16[1024,1024]{1,0:T(8,128)(2,1)S(1)} %bitcast.145, f32[1024,512]{1,0:T(8,128)S(1)} %copy-done.24), kind=kOutput, calls=%fused_computation.45 | convolution fusion | flops 2156396544 | bytes 10485760 | tf_op jit(solution)/shard_map/dot_general | solution.py:181
  53.5 4.4 %fusion.17 = f32[2048,512]{1,0:T(8,128)} fusion(bf16[1024,512]{1,0:T(8,128)(2,1)S(1)} %bitcast.140, bf16[1024,1024]{1,0:T(8,128)(2,1)S(1)} %bitcast.149, bf16[1024,1024]{1,0:T(8,128)(2,1)S(1)} %bitcast.146), kind=kOutput, calls=%fused_computation.43 | convolution fusion | flops 2155872256 | bytes 9437184 | tf_op jit(solution)/shard_map/dot_general | solution.py:181
  58.0 9.6 %all-to-all-done = bf16[128,8,512]{2,0,1:T(8,128)(2,1)} async-done(((bf16[128,8,512]{2,0,1:T(8,128)(2,1)}), bf16[128,8,512]{2,0,1:T(8,128)(2,1)}, u32[]{:S(2)}, u32[]{:S(2)}) %all-to-all-start) | async-done | bytes 1048608 | tf_op jit(solution)/shard_map/all_to_all | solution.py:229
  67.6 5.0 %fusion.18 = f32[2048,512]{1,0:T(8,128)S(1)} fusion(bf16[1024,512]{1,0:T(8,128)(2,1)} %bitcast.9, bf16[1024,1024]{1,0:T(8,128)(2,1)} %bitcast.150, bf16[1024,1024]{1,0:T(8,128)(2,1)} %bitcast.147), kind=kOutput, calls=%fused_computation.44 | convolution fusion | flops 2155872256 | bytes 9437184 | tf_op jit(solution)/shard_map/dot_general | solution.py:181
  72.6 1.2 fusion.28
  73.8 2.2 fusion.30
  76.0 0.2 pad_maximum_fusion.2
  76.2 1.8 pad_maximum_fusion.1
  78.0 1.1 copy-done.3
  79.2 1.3 copy-done.5
  80.4 4.5 %add_convert_fusion.3 = bf16[1024,512]{1,0:T(8,128)(2,1)} fusion(bf16[1024,512]{1,0:T(8,128)(2,1)} %bitcast.9, bf16[2048,512]{1,0:T(8,128)(2,1)S(1)} %bitcast.151, f32[512]{0:T(512)S(1)} %bitcast.161, f32[1024,1024]{1,0:T(8,128)S(1)} %bitcast.136, f32[1024,1024]{1,0:T(8,128)S(1)} %bitcast.132), kind=kOutput, calls=%fused_computation.35 | convolution fusion | flops 2155872256 | bytes 12584960 | tf_op jit(solution)/shard_map/dot_general | solution.py:187
  85.0 3.3 %add_convert_fusion.1 = bf16[1024,512]{1,0:T(8,128)(2,1)} fusion(bf16[1024,512]{1,0:T(8,128)(2,1)S(1)} %bitcast.141, bf16[2048,512]{1,0:T(8,128)(2,1)S(1)} %bitcast.143, f32[512]{0:T(512)S(1)} %bitcast.162, f32[1024,1024]{1,0:T(8,128)S(1)} %bitcast.137, f32[1024,1024]{1,0:T(8,128)S(1)} %bitcast.133), kind=kOutput, calls=%fused_computation.32 | convolution fusion | flops 2155872256 | bytes 12584960 | tf_op jit(solution)/shard_map/dot_general | solution.py:187
  88.3 3.6 %all-to-all-start.3 = ((bf16[8,128,512]{2,1,0:T(8,128)(2,1)}), bf16[8,128,512]{2,1,0:T(8,128)(2,1)S(1)}, u32[]{:S(2)}, u32[]{:S(2)}) async-start(bf16[8,128,512]{2,1,0:T(8,128)(2,1)} %bitcast.154), calls=%async_computation.3 | async-start | bytes 2097152 | tf_op jit(solution)/shard_map/all_to_all | solution.py:253
  91.8 1.6 fusion.64
  93.4 1.6 fusion.63
  95.0 1.6 fusion.62
  96.6 1.6 fusion.61
  98.1 1.6 fusion.60
  99.7 1.6 fusion.59
  101.3 1.6 fusion.58
  102.8 1.6 fusion.57
  104.4 13.2 %all-to-all-done.3 = bf16[8,128,512]{2,1,0:T(8,128)(2,1)S(1)} async-done(((bf16[8,128,512]{2,1,0:T(8,128)(2,1)}), bf16[8,128,512]{2,1,0:T(8,128)(2,1)S(1)}, u32[]{:S(2)}, u32[]{:S(2)}) %all-to-all-start.3) | async-done | bytes 1048608 | tf_op jit(solution)/shard_map/all_to_all | solution.py:253
  117.6 4.2 %all-to-all-start.1 = ((bf16[8,128,512]{2,1,0:T(8,128)(2,1)}), bf16[8,128,512]{2,1,0:T(8,128)(2,1)}, u32[]{:S(2)}, u32[]{:S(2)}) async-start(bf16[8,128,512]{2,1,0:T(8,128)(2,1)} %fusion.57), calls=%async_computation.1 | async-start | bytes 2097152 | tf_op jit(solution)/shard_map/all_to_all | solution.py:12
  121.9 0.3 convert_bitcast_fusion.4
  122.3 1.0 copy-done.8
  123.4 0.3 copy-done.9
  123.7 1.9 fusion.2
  125.6 21.9 %all-to-all-done.1 = bf16[8,128,512]{2,1,0:T(8,128)(2,1)} async-done(((bf16[8,128,512]{2,1,0:T(8,128)(2,1)}), bf16[8,128,512]{2,1,0:T(8,128)(2,1)}, u32[]{:S(2)}, u32[]{:S(2)}) %all-to-all-start.1) | async-done | bytes 1048608 | tf_op jit(solution)/shard_map/all_to_all | solution.py:12
  147.5 2.9 %convert_bitcast_fusion.5 = f32[128,8,512]{2,0,1:T(8,128)} fusion(bf16[8,128,512]{2,1,0:T(8,128)(2,1)} %all-to-all-done.1), kind=kLoop, calls=%fused_computation.27 | loop fusion | flops 524288 | bytes 3145728 | tf_op jit(solution)/shard_map/convert_element_type | solution.py:255
  150.4 2.9 %copy.24 = f32[128,8,512]{0,2,1:T(8,128)} copy(f32[128,8,512]{2,0,1:T(8,128)} %convert_bitcast_fusion.5) | data formatting | bytes 4194304 | tf_op jit(solution)/shard_map/convert_element_type | solution.py:255
  153.3 3.5 %fusion.7 = (bf16[128,4096]{0,1:T(8,128)(2,1)}, bf16[128,4096]{0,1:T(8,128)(2,1)}) fusion(bf16[1,128,4096]{1,2,0:T(8,128)(2,1)S(1)} %copy.25, f32[128,8,512]{0,2,1:T(8,128)} %copy.24, bf16[1,128,4096]{1,2,0:T(8,128)(2,1)S(1)} %copy.22), kind=kLoop, calls=%fused_computation.19 | loop fusion | flops 3145728 | bytes 6291456 | tf_op jit(solution)/shard_map/convert_element_type | solution.py:270
  156.7 0.5 collective-permute-start
  157.2 1.2 collective-permute-start.2
  158.5 0.4 collective-permute-start.1
  158.9 5.8 %multiply_reduce_fusion.1 = (f32[512]{0:T(512)}, f32[1024,512]{1,0:T(8,128)S(1)}) fusion(f32[1024,512]{1,0:T(8,128)} %fusion.12, f32[1024]{0:T(1024)S(1)} %negate_multiply_fusion, bf16[2048,512]{1,0:T(8,128)(2,1)S(1)} %bitcast.144, f32[1024,1024]{1,0:T(8,128)} %bitcast.135, f32[1024,1024]{1,0:T(8,128)S(1)} %bitcast.134), kind=kOutput, calls=%fused_computation.29 | convolution fusion | flops 2155347456 | bytes 14686208 | tf_op jit(solution)/shard_map/dot_general | solution.py:187
  164.7 3.3 %fusion.104 = (f32[64]{0:T(128)S(1)}, f32[1024,64]{0,1:T(8,128)S(1)}) fusion(f32[1024,64]{0,1:T(8,128)S(1)} %copy-done.17, f32[1,64,512]{2,1,0:T(8,128)S(1)} %copy-done, f32[1024,512]{1,0:T(8,128)S(1)} %get-tuple-element.60, f32[1024]{0:T(1024)S(1)} %iota_convert_fusion, f32[512]{0:T(512)S(1)} %bitcast.157), kind=kOutput, calls=%fused_computation.159 | convolution fusion | flops 404881344 | bytes 2758912 | tf_op jit(solution)/shard_map/fc,tc->ft/dot_general | solution.py:23
  168.0 0.4 convolution_bitcast_fusion
  168.4 36.3 %all-reduce = (f32[1,33,64]{2,1,0:T(8,128)S(1)}, f32[1,64]{1,0:T(1,128)}) all-reduce(f32[1,33,64]{2,1,0:T(8,128)S(1)} %convolution_bitcast_fusion, f32[1,64]{1,0:T(1,128)S(1)} %bitcast.160), channel_id=1, replica_groups=mesh['pipe'=4,'seq'=8] {'seq'}, use_global_device_ids=true, to_apply=%region_0.1 | all-reduce | flops 2176 | bytes 17408 | tf_op jit(solution)/shard_map/psum | solution.py:263
  204.7 0.6 copy.30
  205.3 2.2 multiply_reduce_fusion
  207.5 3.4 %fusion.23 = f32[1,64,512]{2,1,0:T(8,128)} fusion(f32[1024,64]{0,1:T(8,128)} %copy-done.16, f32[1024,512]{1,0:T(8,128)S(1)} %copy-done.23, f32[1024]{0:T(1024)S(1)} %iota_convert_fusion, f32[512]{0:T(512)S(1)} %bitcast.158), kind=kOutput, calls=%fused_computation.48 | convolution fusion | flops 404750336 | bytes 2496512 | tf_op jit(solution)/shard_map/ft,tc->fc/dot_general | solution.py:23
  210.9 2.3 %copy.29 = bf16[1,128,4096]{2,1,0:T(8,128)(2,1)} copy(bf16[1,128,4096]{1,2,0:T(8,128)(2,1)} %bitcast.40) | data formatting | bytes 2097152
  213.2 2.3 %copy.28 = bf16[1,128,4096]{2,1,0:T(8,128)(2,1)} copy(bf16[1,128,4096]{1,2,0:T(8,128)(2,1)} %bitcast.25) | data formatting | bytes 2097152
  215.4 1.0 copy.49
  216.4 1.0 copy.50
  (61 shorter events, 0.4 us)
Async XLA Ops:
  0.6 23.8 %copy-start = (f32[1,64,512]{2,1,0:T(8,128)S(1)}, f32[1,64,512]{2,1,0:T(8,128)}, u32[]{:S(2)}) copy-start(f32[1,64,512]{2,1,0:T(8,128)} %param.15) | copy-start | bytes 393220
  0.7 1.7 copy-start.15
  4.7 33.0 %all-to-all-start.2 = ((bf16[128,8,512]{2,0,1:T(8,128)(2,1)}), bf16[128,8,512]{2,0,1:T(8,128)(2,1)S(1)}, u32[]{:S(2)}, u32[]{:S(2)}) async-start(bf16[128,8,512]{2,0,1:T(8,128)(2,1)} %copy.26), calls=%async_computation.2 | async-start | bytes 2097152 | tf_op jit(solution)/shard_map/all_to_all | solution.py:230
  11.9 1.9 copy-start.19
  13.8 2.5 %copy-start.18 = (f32[1,33,64]{2,0,1:T(1,128)S(1)}, f32[1,33,64]{2,0,1:T(1,128)}, u32[]{:S(2)}) copy-start(f32[1,33,64]{2,0,1:T(1,128)} %param.13) | copy-start | bytes 25348
  13.8 2.5 %copy-start.20 = (f32[1,64]{1,0:T(1,128)S(1)}, f32[1,64]{1,0:T(1,128)}, u32[]{:S(2)}) copy-start(f32[1,64]{1,0:T(1,128)} %param.14) | copy-start | bytes 772
  18.3 6.1 %copy-start.16 = (f32[1024,64]{0,1:T(8,128)}, f32[1024,64]{0,1:T(8,128)S(1)}, u32[]{:S(2)}) copy-start(f32[1024,64]{0,1:T(8,128)S(1)} %get-tuple-element.55) | copy-start | bytes 786436
  37.7 47.3 %copy-start.6 = (bf16[128,8,512]{2,0,1:T(8,128)(2,1)}, bf16[128,8,512]{2,0,1:T(8,128)(2,1)S(1)}, u32[]{:S(2)}) copy-start(bf16[128,8,512]{2,0,1:T(8,128)(2,1)S(1)} %all-to-all-done.2) | copy-start | bytes 3145732
  37.7 29.9 %all-to-all-start = ((bf16[128,8,512]{2,0,1:T(8,128)(2,1)}), bf16[128,8,512]{2,0,1:T(8,128)(2,1)}, u32[]{:S(2)}, u32[]{:S(2)}) async-start(bf16[128,8,512]{2,0,1:T(8,128)(2,1)} %copy.23), calls=%async_computation | async-start | bytes 2097152 | tf_op jit(solution)/shard_map/all_to_all | solution.py:229
  42.1 2.6 %copy-start.10 = (f32[128,1024]{1,0:T(8,128)S(1)}, f32[128,1024]{1,0:T(8,128)}, u32[]{:S(2)}) copy-start(f32[128,1024]{1,0:T(8,128)} %get-tuple-element.47) | copy-start | bytes 1572868
  42.2 2.6 %copy-start.11 = (f32[128,1024]{1,0:T(8,128)S(1)}, f32[128,1024]{1,0:T(8,128)}, u32[]{:S(2)}) copy-start(f32[128,1024]{1,0:T(8,128)} %get-tuple-element.48) | copy-start | bytes 1572868
  44.7 8.8 %copy-start.13 = (bf16[8,128,1024]{2,1,0:T(8,128)(2,1)}, bf16[8,128,1024]{2,1,0:T(8,128)(2,1)S(1)}, u32[]{:S(2)}) copy-start(bf16[8,128,1024]{2,1,0:T(8,128)(2,1)S(1)} %get-tuple-element.43) | copy-start | bytes 6291460
  44.7 8.8 %copy-start.14 = (bf16[8,128,1024]{2,1,0:T(8,128)(2,1)}, bf16[8,128,1024]{2,1,0:T(8,128)(2,1)S(1)}, u32[]{:S(2)}) copy-start(bf16[8,128,1024]{2,1,0:T(8,128)(2,1)S(1)} %get-tuple-element.44) | copy-start | bytes 6291460
  44.7 4.4 %copy-start.24 = (f32[1024,512]{1,0:T(8,128)S(1)}, f32[1024,512]{1,0:T(8,128)}, u32[]{:S(2)}) copy-start(f32[1024,512]{1,0:T(8,128)} %fusion.12) | copy-start | bytes 6291460
  67.6 5.0 %copy-start.1 = (f32[2048,512]{1,0:T(8,128)S(1)}, f32[2048,512]{1,0:T(8,128)}, u32[]{:S(2)}) copy-start(f32[2048,512]{1,0:T(8,128)} %fusion.19) | copy-start | bytes 12582916
  67.6 5.0 %copy-start.2 = (f32[2048,512]{1,0:T(8,128)S(1)}, f32[2048,512]{1,0:T(8,128)}, u32[]{:S(2)}) copy-start(f32[2048,512]{1,0:T(8,128)} %fusion.17) | copy-start | bytes 12582916
  76.2 2.9 %copy-start.3 = (f32[8,128,1024]{2,1,0:T(8,128)S(1)}, f32[8,128,1024]{2,1,0:T(8,128)}, u32[]{:S(2)}) copy-start(f32[8,128,1024]{2,1,0:T(8,128)} %get-tuple-element.41) | copy-start | bytes 12582916
  76.2 4.2 %copy-start.5 = (f32[8,128,1024]{2,1,0:T(8,128)S(1)}, f32[8,128,1024]{2,1,0:T(8,128)}, u32[]{:S(2)}) copy-start(f32[8,128,1024]{2,1,0:T(8,128)} %get-tuple-element.42) | copy-start | bytes 12582916
  76.2 4.2 %copy-start.21 = (f32[1,512]{1,0:T(1,128)S(1)}, f32[1,512]{1,0:T(1,128)}, u32[]{:S(2)}) copy-start(f32[1,512]{1,0:T(1,128)} %param.17) | copy-start | bytes 6148
  88.3 29.3 %all-to-all-start.3 = ((bf16[8,128,512]{2,1,0:T(8,128)(2,1)}), bf16[8,128,512]{2,1,0:T(8,128)(2,1)S(1)}, u32[]{:S(2)}, u32[]{:S(2)}) async-start(bf16[8,128,512]{2,1,0:T(8,128)(2,1)} %bitcast.154), calls=%async_computation.3 | async-start | bytes 2097152 | tf_op jit(solution)/shard_map/all_to_all | solution.py:253
  117.6 29.9 %all-to-all-start.1 = ((bf16[8,128,512]{2,1,0:T(8,128)(2,1)}), bf16[8,128,512]{2,1,0:T(8,128)(2,1)}, u32[]{:S(2)}, u32[]{:S(2)}) async-start(bf16[8,128,512]{2,1,0:T(8,128)(2,1)} %fusion.57), calls=%async_computation.1 | async-start | bytes 2097152 | tf_op jit(solution)/shard_map/all_to_all | solution.py:12
  122.1 1.2 copy-start.8
  122.2 1.5 copy-start.9
  153.3 5.6 %copy-start.4 = (f32[8,128,1024]{2,1,0:T(8,128)S(1)}, f32[8,128,1024]{2,1,0:T(8,128)}, u32[]{:S(2)}) copy-start(f32[8,128,1024]{2,1,0:T(8,128)} %get-tuple-element.41) | copy-start | bytes 12582916
  153.3 5.6 %copy-start.12 = (bf16[2,1024,512]{2,1,0:T(8,128)(2,1)S(1)}, bf16[2,1024,512]{2,1,0:T(8,128)(2,1)}, u32[]{:S(2)}) copy-start(bf16[2,1024,512]{2,1,0:T(8,128)(2,1)} %get-tuple-element.62) | copy-start | bytes 6291460
  156.7 54.2 %collective-permute-start.3 = (bf16[128,4096]{0,1:T(8,128)(2,1)}, bf16[128,4096]{0,1:T(8,128)(2,1)}, u32[]{:S(2)}, u32[]{:S(2)}) collective-permute-start(bf16[128,4096]{0,1:T(8,128)(2,1)} %get-tuple-element.37), channel_id=1, source_target_pairs={{0,24},{8,0},{16,8},{24,16},{1,25},{9,1},{17,9},{25,17},{2,26},{10... | collective-permute-start | bytes 3145736 | tf_op jit(solution)/shard_map/ppermute | solution.py:19
  156.7 56.4 %collective-permute-start = (bf16[128,4096]{0,1:T(8,128)(2,1)}, bf16[128,4096]{0,1:T(8,128)(2,1)}, u32[]{:S(2)}, u32[]{:S(2)}) collective-permute-start(bf16[128,4096]{0,1:T(8,128)(2,1)} %get-tuple-element.38), channel_id=1, source_target_pairs={{0,8},{8,16},{16,24},{24,0},{1,9},{9,17},{17,25},{25,1},{2,10},{10... | collective-permute-start | bytes 3145736 | tf_op jit(solution)/shard_map/ppermute | solution.py:19
  157.2 58.2 %collective-permute-start.2 = (bf16[128,4096]{1,0:T(8,128)(2,1)}, bf16[128,4096]{1,0:T(8,128)(2,1)S(1)}, u32[]{:S(2)}, u32[]{:S(2)}) collective-permute-start(bf16[128,4096]{1,0:T(8,128)(2,1)} %get-tuple-element.39), channel_id=1, source_target_pairs={{0,24},{8,0},{16,8},{24,16},{1,25},{9,1},{17,9},{25,17},{2,26},{10... | collective-permute-start | bytes 3145736 | tf_op jit(solution)/shard_map/ppermute | solution.py:19
  158.5 57.0 %collective-permute-start.1 = (bf16[128,4096]{1,0:T(8,128)(2,1)}, bf16[128,4096]{1,0:T(8,128)(2,1)S(1)}, u32[]{:S(2)}, u32[]{:S(2)}) collective-permute-start(bf16[128,4096]{1,0:T(8,128)(2,1)} %get-tuple-element.40), channel_id=1, source_target_pairs={{0,24},{8,0},{16,8},{24,16},{1,25},{9,1},{17,9},{25,17},{2,26},{10... | collective-permute-start | bytes 3145736 | tf_op jit(solution)/shard_map/ppermute | solution.py:19
  158.9 5.8 %copy-start.17 = (f32[1024,64]{0,1:T(8,128)S(1)}, f32[1024,64]{0,1:T(8,128)}, u32[]{:S(2)}) copy-start(f32[1024,64]{0,1:T(8,128)} %get-tuple-element.56) | copy-start | bytes 786436
  164.7 3.7 %copy-start.22 = (f32[1024,512]{1,0:T(8,128)}, f32[1024,512]{1,0:T(8,128)S(1)}, u32[]{:S(2)}) copy-start(f32[1024,512]{1,0:T(8,128)S(1)} %get-tuple-element.60) | copy-start | bytes 6291460
  164.7 40.6 %copy-start.7 = (bf16[128,8,512]{2,0,1:T(8,128)(2,1)S(1)}, bf16[128,8,512]{2,0,1:T(8,128)(2,1)}, u32[]{:S(2)}) copy-start(bf16[128,8,512]{2,0,1:T(8,128)(2,1)} %copy-done.6) | copy-start | bytes 3145732
  204.7 2.8 %copy-start.23 = (f32[1024,512]{1,0:T(8,128)S(1)}, f32[1024,512]{1,0:T(8,128)}, u32[]{:S(2)}) copy-start(f32[1024,512]{1,0:T(8,128)} %copy-done.22) | copy-start | bytes 6291460
